TPU v7x, 512 devices: a whole 4x4x16 slice. The times are simulated.
512 devices in a mesh: gx: 64 (over y, z), ta: 8 (over x, core).
Axes of the slice: x: 4, y: 4, z: 16, core: 2. Of those that a mesh axis runs over, the one named last changes fastest.
Arguments:
- query_vecs: bfloat16 [256, 64, 5120], P('gx', None, 'ta'), may hold values from -32 to 32
- key_vecs: bfloat16 [256, 64, 5120], P('gx', None, 'ta'), may hold values from -6 to 6
- value_vecs: bfloat16 [256, 64, 5120], P('gx', None, 'ta'), may hold values from -6 to 6
- slot_map: int32 [16, 64], replicated, may hold values from 0 to 63, each once within a row
- edge_list: int32 [256, 2], replicated, may hold values from 0 to 63
- edge_types: int32 [256], replicated, may hold values from 0 to 2
- type_gain: float32 [2, 3, 5120], P(None, None, 'ta'), may hold values from 0.25 to 2
- norm_gain: float32 [2, 5120], P(None, 'ta'), may hold values from 0.5 to 2
- gate_proj: bfloat16 [2, 5120, 20480], P(None, 'ta', 'gx'), may hold values from -0.078125 to 0.078125
- up_proj: bfloat16 [2, 5120, 20480], P(None, 'ta', 'gx'), may hold values from -0.078125 to 0.078125
- down_proj: bfloat16 [2, 20480, 5120], P(None, 'gx', 'ta'), may hold values from -0.0390625 to 0.0390625
Outputs:
- node_states: bfloat16 [512, 5120], P('gx', 'ta')
All inputs are finite; a program needn't handle non-finite values.
Results may differ from a plain program's by a relative error of at most 0.04.
Values may be sent and summed in bfloat16 or wider, within the bound.
A program may use at most 64 MiB of HBM per device.

v0:
```python
import jax
import jax.numpy as jnp
from jax import lax
from jax.sharding import PartitionSpec as P

D = 5120
HEAD_DIM = 128
VENUES = 16
STEPS = 16
NODE_STEPS = 8
ROUNDS = 2
ETYPES = 3


def settle_rows(nodes, hidden, down_local, row_begin, rows_dev):
    summed = lax.psum_scatter(
        jnp.dot(hidden, down_local, preferred_element_type=jnp.float32),
        "gx",
        scatter_dimension=0,
        tiled=True,
    )
    base_rows = lax.dynamic_slice_in_dim(nodes, row_begin, rows_dev, 0)
    return (base_rows.astype(jnp.float32) + summed).astype(jnp.bfloat16)


def per_device(
    query_vecs,
    key_vecs,
    value_vecs,
    slot_map,
    edge_list,
    edge_types,
    type_gain,
    norm_gain,
    gate_proj,
    up_proj,
    down_proj,
):
    pairs_dev = query_vecs.shape[0]
    inst_total = query_vecs.shape[1]
    feat_width = query_vecs.shape[2]
    head_count = feat_width // HEAD_DIM
    gx_count = lax.axis_size("gx")
    inst_local = inst_total // gx_count
    score_scale = 1.0 / HEAD_DIM**0.5
    venue_idx = lax.axis_index("gx") * pairs_dev // STEPS
    slot_order = lax.dynamic_index_in_dim(slot_map, venue_idx, 0, keepdims=False)
    split_shape = (pairs_dev, gx_count, inst_local, feat_width)
    sorted_queries = jnp.take(query_vecs, slot_order, axis=1).reshape(split_shape)
    sorted_keys = jnp.take(key_vecs, slot_order, axis=1).reshape(split_shape)
    sorted_values = jnp.take(value_vecs, slot_order, axis=1).reshape(split_shape)
    query_steps = jnp.arange(VENUES * NODE_STEPS) % NODE_STEPS + (STEPS - NODE_STEPS)
    key_steps = jnp.arange(VENUES * STEPS) % STEPS
    allowed = key_steps[None, :] <= query_steps[:, None]
    queries = lax.all_to_all(sorted_queries, "gx", split_axis=1, concat_axis=0, tiled=True)
    keyset = lax.all_to_all(sorted_keys, "gx", split_axis=1, concat_axis=0, tiled=True)
    valueset = lax.all_to_all(sorted_values, "gx", split_axis=1, concat_axis=0, tiled=True)
    pair_total = queries.shape[0]
    item_count = queries.shape[2]
    queries = queries.reshape(VENUES, STEPS, item_count, head_count, HEAD_DIM)[
        :, STEPS - NODE_STEPS :
    ]
    queries = queries.reshape(VENUES * NODE_STEPS, item_count, head_count, HEAD_DIM)
    keyset = keyset.reshape(pair_total, item_count, head_count, HEAD_DIM)
    valueset = valueset.reshape(pair_total, item_count, head_count, HEAD_DIM)
    scores = (
        jnp.einsum("qnhd,knhd->nhqk", queries, keyset, preferred_element_type=jnp.float32)
        * score_scale
    )
    scores = jnp.where(allowed[None, None], scores, jnp.float32(-1e30))
    row_max = jnp.max(scores, axis=-1, keepdims=True)
    expd = jnp.exp(scores - row_max)
    probs = (expd / jnp.sum(expd, axis=-1, keepdims=True)).astype(jnp.bfloat16)
    attended = jnp.einsum("nhqk,knhd->nqhd", probs, valueset, preferred_element_type=jnp.float32)
    attended = attended.reshape(item_count, VENUES, NODE_STEPS, feat_width)
    pooled = jnp.mean(attended, axis=1).astype(jnp.bfloat16)
    own_rows = pooled.reshape(inst_local * NODE_STEPS, feat_width)
    rows_dev = own_rows.shape[0]
    row_begin = lax.axis_index("gx") * rows_dev
    nodes = lax.all_gather(own_rows, "gx", axis=0, tiled=True)
    row_total = nodes.shape[0]
    node_ids = jnp.arange(inst_total)
    type_ids = jnp.arange(ETYPES)
    at_source = (edge_list[:, 0][:, None] == node_ids[None, :]).astype(jnp.float32)
    at_target = (edge_list[:, 1][:, None] == node_ids[None, :]).astype(jnp.float32)
    of_type = (edge_types[:, None] == type_ids[None, :]).astype(jnp.float32)
    adjacency = jnp.einsum("et,ei,ej->tij", of_type, at_target, at_source)
    degree = jnp.maximum(jnp.sum(at_target, axis=0), 1.0)
    adj_rows = adjacency.reshape(ETYPES * inst_total, inst_total).astype(jnp.bfloat16)
    for layer_idx in range(ROUNDS):
        flat_nodes = nodes.reshape(inst_total, NODE_STEPS * feat_width)
        gathered = jnp.dot(adj_rows, flat_nodes, preferred_element_type=jnp.float32)
        gathered = gathered.reshape(ETYPES, inst_total, NODE_STEPS, feat_width)
        message = (
            jnp.sum(gathered * type_gain[layer_idx][:, None, None, :], axis=0)
            / degree[:, None, None]
        )
        pre_norm = nodes.astype(jnp.float32) + message.reshape(row_total, feat_width)
        squares = lax.psum(jnp.sum(pre_norm * pre_norm, axis=-1), "ta")
        row_scale = lax.rsqrt(squares / D + 1e-05)[:, None]
        normed = (pre_norm * row_scale * norm_gain[layer_idx][None, :]).astype(jnp.bfloat16)
        gate_part = jnp.dot(normed, gate_proj[layer_idx], preferred_element_type=jnp.float32)
        up_part = jnp.dot(normed, up_proj[layer_idx], preferred_element_type=jnp.float32)
        gate_sum, up_sum = (
            lax.psum(gate_part.astype(jnp.bfloat16), "ta").astype(jnp.float32),
            lax.psum(up_part.astype(jnp.bfloat16), "ta").astype(jnp.float32),
        )
        hidden = (jax.nn.silu(gate_sum) * up_sum).astype(jnp.bfloat16)
        down_local = down_proj[layer_idx]
        if layer_idx == ROUNDS - 1:
            own_rows = settle_rows(nodes, hidden, down_local, row_begin, rows_dev)
        else:
            own_rows = settle_rows(nodes, hidden, down_local, row_begin, rows_dev)
            nodes = lax.all_gather(own_rows, "gx", axis=0, tiled=True)
    return own_rows


def solution(mesh):
    placed = (
        P("gx", None, "ta"),
        P("gx", None, "ta"),
        P("gx", None, "ta"),
        P(),
        P(),
        P(),
        P(None, None, "ta"),
        P(None, "ta"),
        P(None, "ta", "gx"),
        P(None, "ta", "gx"),
        P(None, "gx", "ta"),
    )
    return jax.shard_map(
        per_device, mesh=mesh, in_specs=placed, out_specs=P("gx", "ta"), check_vma=False
    )
```

profile of v0, /device:TPU:1, one launch (start us, length us, event | category | flops | bytes accessed | tf_op | source)
XLA Modules:
  0.0 1040.7 jit_solution(5708310502350677954)
XLA Ops:
  6.5 0.7 compare_and_fusion
  7.3 0.2 copy-done
  7.5 1.6 gather_fusion
  9.1 0.0 copy-start.2
  9.1 1.6 gather_fusion.1
  10.8 1.6 gather_fusion.2
  12.4 0.2 select_bitcast_fusion.1
  12.5 1.0 copy.32
  13.5 19.4 %all-to-all-start.1 = ((bf16[4,64,1,640]{3,0,2,1:T(4,128)(2,1)}), bf16[4,64,1,640]{3,0,2,1:T(4,128)(2,1)S(1)}, u32[]{:S(2)}, u32[]{:S(2)}) async-start(bf16[4,64,1,640]{3,0,2,1:T(4,128)(2,1)} %copy.32), calls=%async_computation.1 | async-start | bytes 655360 | tf_op jit(solution)/shard_map/all_to_all | solution.py:55
  33.0 0.0 copy-start.9
  33.0 1.0 copy.34
  33.9 20.9 %all-to-all-done.1 = bf16[4,64,1,640]{3,0,2,1:T(4,128)(2,1)S(1)} async-done(((bf16[4,64,1,640]{3,0,2,1:T(4,128)(2,1)}), bf16[4,64,1,640]{3,0,2,1:T(4,128)(2,1)S(1)}, u32[]{:S(2)}, u32[]{:S(2)}) %all-to-all-start.1) | async-done | bytes 327712 | tf_op jit(solution)/shard_map/all_to_all | solution.py:55
  54.8 7.7 all-to-all-start.2
  62.5 1.0 copy.31
  63.5 0.0 copy-done.6
  63.5 0.1 fusion.49
  63.6 0.1 div.63
  63.7 0.1 div.64
  63.8 19.6 %all-to-all-done.2 = bf16[4,64,1,640]{3,0,2,1:T(4,128)(2,1)S(1)} async-done(((bf16[4,64,1,640]{3,0,2,1:T(4,128)(2,1)}), bf16[4,64,1,640]{3,0,2,1:T(4,128)(2,1)S(1)}, u32[]{:S(2)}, u32[]{:S(2)}) %all-to-all-start.2) | async-done | bytes 327712 | tf_op jit(solution)/shard_map/all_to_all | solution.py:56
  83.4 8.0 all-to-all-start
  91.4 0.0 all-reduce.15.cloned.1.call-start
  91.5 0.2 fusion.6
  91.6 0.1 broadcast_compare_fusion
  91.7 0.1 reshape.143
  91.9 0.1 slice.58
  91.9 0.1 reshape.146
  92.1 0.5 fusion.68
  92.5 0.3 fusion.5
  92.8 19.3 %all-to-all-done = bf16[4,64,1,640]{3,0,2,1:T(4,128)(2,1)S(1)} async-done(((bf16[4,64,1,640]{3,0,2,1:T(4,128)(2,1)}), bf16[4,64,1,640]{3,0,2,1:T(4,128)(2,1)S(1)}, u32[]{:S(2)}, u32[]{:S(2)}) %all-to-all-start) | async-done | bytes 327712 | tf_op jit(solution)/shard_map/all_to_all | solution.py:57
  112.1 0.1 reshape.141
  112.2 1.4 convolution_bitcast_fusion
  113.6 0.2 copy.37
  113.8 0.1 reshape.147
  114.0 74.0 %all_gather.6 = bf16[512,640]{1,0:T(8,128)(2,1)S(1)} all-gather(bf16[8,640]{1,0:T(8,128)(2,1)S(1)} %multiply_convert_fusion.2), channel_id=1, replica_groups=mesh['gx'=64,'ta'=8] {'gx'}, dimensions={0}, use_global_device_ids=true | all-gather | bytes 665600 | tf_op jit(solution)/shard_map/all_gather | solution.py:80
  188.0 0.3 reshape.148
  188.3 0.7 multiply_reduce_fusion.1
  189.0 0.0 copy-start.3
  189.0 0.9 multiply_reduce_fusion.3
  189.9 41.5 %psum.42 = f32[512]{0:T(512)S(1)} all-reduce(f32[512]{0:T(512)S(1)} %get-tuple-element.14), channel_id=1, replica_groups=mesh['gx'=64,'ta'=8] {'ta'}, use_global_device_ids=true, to_apply=%region_6.8 | all-reduce | flops 512 | bytes 4096 | tf_op jit(solution)/shard_map/psum | solution.py:99
  231.4 1.3 convolution_convert_fusion.3
  232.7 1.3 convolution_convert_fusion.2
  233.9 0.0 all-reduce.15.cloned.1.call-update
  234.0 0.0 all-reduce.9.cloned.1.call-start
  234.0 65.2 %all-reduce.15.cloned.1.call-done = (bf16[512,320]{0,1:T(8,128)(2,1)}, bf16[512,320]{0,1:T(8,128)(2,1)}) async-done(((bf16[512,320]{0,1:T(8,128)(2,1)}, bf16[512,320]{0,1:T(8,128)(2,1)}), (bf16[512,320]{0,1:T(8,128)(2,1)}, bf16[512,320]{0,1:T(8,128)(2,1)})) %all-reduce.15.cloned.1.call-update) | async-done | bytes 655376 | tf_op jit(solution)/shard_map/psum | solution.py:106
  299.3 2.9 fusion.23
  302.2 0.0 all-reduce.9.cloned.1.call-update
  302.2 0.0 all-reduce.13.cloned.1.call-start
  302.3 1.3 dynamic-slice
  304.2 265.0 %all-reduce.9.cloned.1.call-done = f32[512,640]{1,0:T(8,128)} async-done(((f32[512,640]{1,0:T(8,128)}), f32[512,640]{1,0:T(8,128)}) %all-reduce.9.cloned.1.call-update) | async-done | bytes 1310736
  569.2 0.7 fusion.51
  570.0 73.1 %all_gather.7 = bf16[512,640]{1,0:T(8,128)(2,1)S(1)} all-gather(bf16[8,640]{1,0:T(8,128)(2,1)S(1)} %fusion.51), channel_id=1, replica_groups=mesh['gx'=64,'ta'=8] {'gx'}, dimensions={0}, use_global_device_ids=true | all-gather | bytes 665600 | tf_op jit(solution)/shard_map/all_gather | solution.py:114
  643.1 0.3 reshape.149
  643.4 0.7 multiply_reduce_fusion
  644.1 0.9 multiply_reduce_fusion.2
  645.0 47.5 %psum.45 = f32[512]{0:T(512)S(1)} all-reduce(f32[512]{0:T(512)S(1)} %get-tuple-element.12), channel_id=1, replica_groups=mesh['gx'=64,'ta'=8] {'ta'}, use_global_device_ids=true, to_apply=%region_12.14 | all-reduce | flops 512 | bytes 4096 | tf_op jit(solution)/shard_map/psum | solution.py:99
  692.5 1.3 convolution_convert_fusion.1
  693.8 1.2 convolution_convert_fusion
  695.0 0.0 all-reduce.13.cloned.1.call-update
  695.0 0.0 all-reduce.11.cloned.1.call-start
  695.1 67.9 %all-reduce.13.cloned.1.call-done = (bf16[512,320]{0,1:T(8,128)(2,1)}, bf16[512,320]{0,1:T(8,128)(2,1)}) async-done(((bf16[512,320]{0,1:T(8,128)(2,1)}, bf16[512,320]{0,1:T(8,128)(2,1)}), (bf16[512,320]{0,1:T(8,128)(2,1)}, bf16[512,320]{0,1:T(8,128)(2,1)})) %all-reduce.13.cloned.1.call-update) | async-done | bytes 655376 | tf_op jit(solution)/shard_map/psum | solution.py:106
  763.0 2.8 fusion.19
  765.8 0.0 all-reduce.11.cloned.1.call-update
  765.8 267.0 %all-reduce.11.cloned.1.call-done = f32[512,640]{1,0:T(8,128)} async-done(((f32[512,640]{1,0:T(8,128)}), f32[512,640]{1,0:T(8,128)}) %all-reduce.11.cloned.1.call-update) | async-done | bytes 1310736
  1032.8 1.3 fusion.50
  (32 shorter events, 0.2 us)
Async XLA Ops:
  6.5 1.0 copy-start
  7.5 1.6 copy-start.1
  9.1 1.6 copy-start.2
  13.5 49.9 %copy-start.6 = (f32[2,3,640]{2,0,1:T(2,128)S(1)}, f32[2,3,640]{2,0,1:T(2,128)}, u32[]{:S(2)}) copy-start(f32[2,3,640]{2,0,1:T(2,128)} %param.19) | copy-start | bytes 46084
  13.5 50.0 %copy-start.8 = (s32[256,2]{0,1:T(2,128)S(1)}, s32[256,2]{0,1:T(2,128)}, u32[]{:S(2)}) copy-start(s32[256,2]{0,1:T(2,128)} %param.17) | copy-start | bytes 6148
  13.5 50.3 %copy-start.7 = (f32[2,640]{1,0:T(2,128)S(1)}, f32[2,640]{1,0:T(2,128)}, u32[]{:S(2)}) copy-start(f32[2,640]{1,0:T(2,128)} %param.20) | copy-start | bytes 15364
  13.5 41.3 %all-to-all-start.1 = ((bf16[4,64,1,640]{3,0,2,1:T(4,128)(2,1)}), bf16[4,64,1,640]{3,0,2,1:T(4,128)(2,1)S(1)}, u32[]{:S(2)}, u32[]{:S(2)}) async-start(bf16[4,64,1,640]{3,0,2,1:T(4,128)(2,1)} %copy.32), calls=%async_computation.1 | async-start | bytes 655360 | tf_op jit(solution)/shard_map/all_to_all | solution.py:55
  33.0 58.5 %copy-start.9 = (s32[256]{0:T(256)S(1)}, s32[256]{0:T(256)}, u32[]{:S(2)}) copy-start(s32[256]{0:T(256)} %param.18) | copy-start | bytes 3076
  54.8 28.6 %all-to-all-start.2 = ((bf16[4,64,1,640]{3,0,2,1:T(4,128)(2,1)}), bf16[4,64,1,640]{3,0,2,1:T(4,128)(2,1)S(1)}, u32[]{:S(2)}, u32[]{:S(2)}) async-start(bf16[4,64,1,640]{3,0,2,1:T(4,128)(2,1)} %copy.34), calls=%async_computation.2 | async-start | bytes 655360 | tf_op jit(solution)/shard_map/all_to_all | solution.py:56
  83.4 28.7 %all-to-all-start = ((bf16[4,64,1,640]{3,0,2,1:T(4,128)(2,1)}), bf16[4,64,1,640]{3,0,2,1:T(4,128)(2,1)S(1)}, u32[]{:S(2)}, u32[]{:S(2)}) async-start(bf16[4,64,1,640]{3,0,2,1:T(4,128)(2,1)} %copy.31), calls=%async_computation | async-start | bytes 655360 | tf_op jit(solution)/shard_map/all_to_all | solution.py:57
  91.4 207.9 %all-reduce.15.cloned.1.call-start = ((), (), s32[]{:S(2)}) async-start(), calls=%async_computation.6 | async-start | bytes 1310720 | tf_op jit(solution)/shard_map/psum | solution.py:106
  189.0 42.5 %copy-start.3 = (bf16[2,640,320]{1,2,0:T(8,128)(2,1)S(1)}, bf16[2,640,320]{1,2,0:T(8,128)(2,1)}, u32[]{:S(2)}) copy-start(bf16[2,640,320]{1,2,0:T(8,128)(2,1)} %param.21) | copy-start | bytes 2457604
  231.4 1.3 copy-start.4
  234.0 335.3 %all-reduce.9.cloned.1.call-start = ((), (), s32[]{:S(2)}) async-start(), calls=%async_computation.3 | async-start | bytes 2621440
  302.2 460.8 %all-reduce.13.cloned.1.call-start = ((), (), s32[]{:S(2)}) async-start(), calls=%async_computation.5 | async-start | bytes 1310720 | tf_op jit(solution)/shard_map/psum | solution.py:106
  692.5 1.3 copy-start.5
  693.8 69.3 %copy-start.10 = (bf16[2,320,640]{2,1,0:T(8,128)(2,1)S(1)}, bf16[2,320,640]{2,1,0:T(8,128)(2,1)}, u32[]{:S(2)}) copy-start(bf16[2,320,640]{2,1,0:T(8,128)(2,1)} %param.23) | copy-start | bytes 2457604
  695.0 337.8 %all-reduce.11.cloned.1.call-start = ((), (), s32[]{:S(2)}) async-start(), calls=%async_computation.4 | async-start | bytes 2621440
Sparse Core Ops, SparseCore 0:
  234.1 65.1 all-reduce.14
  302.6 266.5 all-reduce.8
  695.1 67.8 all-reduce.12
  766.2 266.5 all-reduce.10
where the time goes:
time: 1050 us; the launch traced here: 1040 us
  waiting for transfers between devices  725 us (69%)
  blocking collectives  236 us (22%)
  starting transfers between devices  35.2 us (3%)
  matrix products  14.3 us (1%)
  between operations  14.1 us (1%)
  local copies, waits for them, and re-layouts  10.9 us (1%)
    unnamed x6, waiting for transfers between devices  532 us
    all_gather x2, blocking collectives, per_device(): nodes = lax.all_gather(own_rows, 'gx', axis=0, tiled=True)  147 us
    psum x2, waiting for transfers between devices, per_device(): lax.psum(up_part.astype(jnp.bfloat16), 'ta').astype(jnp.float32)  133 us
    psum x2, blocking collectives, per_device(): squares = lax.psum(jnp.sum(pre_norm * pre_norm, axis=-1), 'ta')  89 us
  transfers between devices with their start and end apart: 7, of which 7 were waited for; matrix products, arithmetic and copies ran while one was open for 0% of the time, Pallas kernels for 0%

commit v1 on v0

v1 whole, which is shorter than its diff:
```python
import functools

import jax
import jax.numpy as jnp
from jax import lax
from jax.experimental import pallas as pl
from jax.experimental.pallas import tpu as pltpu
from jax.sharding import PartitionSpec as P

MESH = pl.DeviceIdType.MESH
HEAD = 128
STEPS = 16
NSTEP = 8
ROUNDS = 2
ETYPES = 3
PD = 4
NZ = 16
NC = 2
F32 = jnp.float32
BF16 = jnp.bfloat16


def iota(shape, dim):
    return lax.broadcasted_iota(jnp.int32, shape, dim)


def kernel(
    gx,
    ta,
    q_hbm,
    k_hbm,
    v_hbm,
    slot_ref,
    edge_rows_ref,
    edge_cols_ref,
    tgain_ref,
    ngain_ref,
    g_hbm,
    u_hbm,
    d_hbm,
    out_ref,
    x_in,
    kv_send,
    kv_recv,
    q_send,
    q_recv,
    q_f32,
    gu_in,
    w_ref,
    d_ref,
    adj_ref,
    deg_ref,
    node_ref,
    part_ref,
    s_ref,
    yr_ref,
    zs_ref,
    zr_ref,
    gu_ref,
    cs_ref,
    cr_ref,
    xs_ref,
    xr_ref,
    sq_ref,
    sqr_ref,
    h_ref,
    in_sem,
    w_sem,
    kv_sems,
    q_sems,
    n_send,
    n_z,
    n_y,
    r_send,
    r_y,
    r_z,
    c_send,
    c_core,
    c_x,
    sq_sems,
    h_send,
    h_x,
    h_core,
):
    inst = gx
    nz = NZ if gx >= NZ else gx // 2
    ny = gx // nz
    nx = ta // NC
    feat = out_ref.shape[1]
    heads = feat // HEAD
    ffd = feat // 2
    rows = inst * NSTEP
    ch = rows // ta
    half = rows // 2
    me = lax.axis_index("gx")
    ti = lax.axis_index("ta")
    my_y, my_z = me // nz, me % nz
    my_x, my_c = ti // NC, ti % NC

    def gdev(y, z):
        return (y * nz + z, ti)

    barrier = pltpu.get_barrier_semaphore()

    def greet_gx(k, _):
        pl.semaphore_signal(
            barrier, inc=1, device_id=((me + k) % gx, ti), device_id_type=MESH
        )
        return 0

    lax.fori_loop(1, gx, greet_gx, 0)

    def greet_ta(k, _):
        pl.semaphore_signal(
            barrier, inc=1, device_id=(me, (ti + k) % ta), device_id_type=MESH
        )
        return 0

    lax.fori_loop(1, ta, greet_ta, 0)

    loads = [
        pltpu.make_async_copy(src, x_in.at[i], in_sem.at[i])
        for i, src in enumerate((q_hbm, k_hbm, v_hbm))
    ]
    loads[1].start()
    loads[2].start()
    loads[0].start()
    weights = [
        pltpu.make_async_copy(g_hbm, gu_in.at[0], w_sem.at[0]),
        pltpu.make_async_copy(u_hbm, gu_in.at[1], w_sem.at[1]),
        pltpu.make_async_copy(d_hbm, d_ref.at[:, pl.ds(0, ffd)], w_sem.at[2]),
    ]
    for w in weights:
        w.start()

    order = slot_ref[pl.ds(me * PD // STEPS, 1), :].astype(F32)
    r8 = iota((rows, inst), 0)
    pick = jnp.where(iota((rows, inst), 1) == r8 // NSTEP, order, 0.0)
    slot_of = jnp.sum(pick, axis=1, keepdims=True).astype(jnp.int32)
    row = iota((rows, 2 * PD * inst), 0)
    col = iota((rows, 2 * PD * inst), 1)
    perm = jnp.where(col == (row % NSTEP) * inst + slot_of, 1.0, 0.0).astype(BF16)

    loads[1].wait()
    loads[2].wait()
    keyvals = x_in[1:3].reshape(2 * PD * inst, feat)
    kv_send[...] = (
        jnp.dot(perm, keyvals, preferred_element_type=F32)
        .reshape(inst, NSTEP, feat)
        .astype(BF16)
    )
    loads[0].wait()
    queries = x_in[0].reshape(PD * inst, feat)
    q_send[...] = (
        jnp.dot(perm[:, : PD * inst], queries, preferred_element_type=F32)
        .reshape(inst, NSTEP, feat)[:, :PD]
        .astype(BF16)
    )
    pl.semaphore_wait(barrier, gx - 1 + ta - 1)

    def q_slot(g):
        return (g // 4) * 2 + g % 4 - 2

    has_q = me % 4 >= 2

    @pl.when(has_q)
    def _():
        def send_q(k, _):
            dest = (me + k) % gx
            pltpu.make_async_remote_copy(
                src_ref=q_send.at[dest],
                dst_ref=q_recv.at[q_slot(me)],
                send_sem=q_sems.at[0],
                recv_sem=q_sems.at[1],
                device_id=(dest, ti),
                device_id_type=MESH,
            ).start()
            return 0

        lax.fori_loop(1, gx, send_q, 0)
        pltpu.make_async_copy(
            q_send.at[me], q_recv.at[q_slot(me)], q_sems.at[1]
        ).start()

    def send_kv(k, _):
        dest = (me + k) % gx
        pltpu.make_async_remote_copy(
            src_ref=kv_send.at[dest],
            dst_ref=kv_recv.at[me],
            send_sem=kv_sems.at[0],
            recv_sem=kv_sems.at[1],
            device_id=(dest, ti),
            device_id_type=MESH,
        ).start()
        return 0

    lax.fori_loop(1, gx, send_kv, 0)
    pltpu.make_async_copy(kv_send.at[me], kv_recv.at[me], kv_sems.at[1]).start()

    tgt = edge_rows_ref[1:2, :]
    typ = edge_rows_ref[2:3, :]
    src = edge_cols_ref[:, 0:1]
    edges = tgt.shape[1]
    at_target = iota((rows, edges), 0) // NSTEP == tgt
    at_source = jnp.where(src == iota((edges, rows), 1) // NSTEP, 1.0, 0.0).astype(BF16)
    same_step = iota((rows, rows), 0) % NSTEP == iota((rows, rows), 1) % NSTEP
    for t in range(ETYPES):
        hit = jnp.where(at_target & (typ == t), 1.0, 0.0).astype(BF16)
        count = jnp.dot(hit, at_source, preferred_element_type=F32)
        adj_ref[t] = jnp.where(same_step, count, 0.0).astype(BF16)
    degree = jnp.sum(jnp.where(at_target, 1.0, 0.0), axis=1, keepdims=True)
    deg_ref[...] = jnp.broadcast_to(jnp.maximum(degree, 1.0), deg_ref.shape)

    for w in weights:
        w.wait()
    left = jnp.where(iota((ffd, feat), 0) == iota((ffd, feat), 1), 1.0, 0.0).astype(BF16)
    right = jnp.where(iota((ffd, feat), 0) + ffd == iota((ffd, feat), 1), 1.0, 0.0)
    right = right.astype(BF16)

    def place(r, _):
        w_ref[r] = (
            jnp.dot(gu_in[0, r], left, preferred_element_type=F32)
            + jnp.dot(gu_in[1, r], right, preferred_element_type=F32)
        ).astype(BF16)
        if d_ref.shape[1] > ffd:
            d_ref[r, ffd:, :] = jnp.zeros((d_ref.shape[1] - ffd, feat), BF16)
        return 0

    lax.fori_loop(0, ROUNDS, place, 0)

    pltpu.make_async_copy(q_recv, q_recv, q_sems.at[1]).wait()
    for j in range(q_recv.shape[0]):
        q_f32[j * PD : (j + 1) * PD, :] = q_recv[j].astype(F32)
    q_all = q_f32[...].astype(BF16)
    pltpu.make_async_copy(kv_recv, kv_recv, kv_sems.at[1]).wait()
    kv_all = kv_recv[...].astype(F32).reshape(rows, feat).astype(BF16)
    nq = q_all.shape[0]
    lane = iota((nq, rows), 1)
    key_step = (lane // NSTEP) % 4 * PD + lane % NSTEP
    q_step = iota((nq, rows), 0) % NSTEP + (STEPS - NSTEP)
    allowed = (lane % NSTEP < PD) & (key_step <= q_step)
    pooled = []
    for h in range(heads):
        cut = slice(h * HEAD, (h + 1) * HEAD)
        scores = lax.dot_general(
            q_all[:, cut],
            kv_all[:, cut],
            (((1,), (1,)), ((), ())),
            preferred_element_type=F32,
        ) * (1.0 / HEAD**0.5)
        scores = jnp.where(allowed, scores, -1e30)
        expd = jnp.exp(scores - jnp.max(scores, axis=1, keepdims=True))
        probs = expd / jnp.sum(expd, axis=1, keepdims=True)
        probs = pltpu.roll(probs, PD, 1).astype(BF16)
        att = jnp.dot(probs, kv_all[:, cut], preferred_element_type=F32)
        pooled.append(jnp.mean(att.reshape(nq // NSTEP, NSTEP, HEAD), axis=0))
    node_ref[0, me] = jnp.concatenate(pooled, axis=1).astype(BF16)

    eye = iota((rows, ch), 0) % ch == iota((rows, ch), 1)

    def one_round(r, _):
        nodes = node_ref.at[r]

        def send_z(j, _):
            k = jnp.where(j % 2 == 1, nz // 2 - j // 2, nz // 2 + j // 2)
            pltpu.make_async_remote_copy(
                src_ref=nodes.at[me],
                dst_ref=nodes.at[me],
                send_sem=n_send.at[r],
                recv_sem=n_z.at[r, k],
                device_id=gdev(my_y, (my_z + k) % nz),
                device_id_type=MESH,
            ).start()
            return 0

        lax.fori_loop(1, nz, send_z, 0)

        def pass_on(blk):
            for dy in range(1, ny):
                pltpu.make_async_remote_copy(
                    src_ref=nodes.at[blk],
                    dst_ref=nodes.at[blk],
                    send_sem=n_send.at[r],
                    recv_sem=n_y.at[r],
                    device_id=gdev((my_y + dy) % ny, my_z),
                    device_id_type=MESH,
                ).start()

        pass_on(me)

        def forward(j, _):
            k = jnp.where(j % 2 == 1, (j + 1) // 2, nz - j // 2)
            blk = my_y * nz + (my_z + nz - k) % nz
            pltpu.make_async_copy(nodes.at[blk], nodes.at[blk], n_z.at[r, k]).wait()
            pass_on(blk)
            return 0

        lax.fori_loop(1, nz, forward, 0)
        arrived = nodes.at[pl.ds(0, (ny - 1) * nz)]
        pltpu.make_async_copy(arrived, arrived, n_y.at[r]).wait()

        node_f32 = nodes[...].astype(F32).reshape(rows, feat)
        node_all = node_f32.astype(BF16)
        tgain = tgain_ref[r]
        squares = []
        for m in range(2):
            mine = slice(m * half, (m + 1) * half)
            total = jnp.zeros((half, feat), F32)
            for t in range(ETYPES):
                total += tgain[t : t + 1] * jnp.dot(
                    adj_ref[t, mine, :], node_all, preferred_element_type=F32
                )
            pre = node_f32[mine] + total / deg_ref[mine, 0:1]
            squares.append(jnp.sum(pre * pre, axis=1, keepdims=True))
            scaled = (pre * ngain_ref[pl.ds(r, 1), :]).astype(BF16)
            gu_ref[pl.ds(m * (ta // 2), ta // 2)] = jnp.dot(
                scaled, w_ref[r], preferred_element_type=F32
            ).reshape(ta // 2, ch, feat)
        square = jnp.concatenate(squares, axis=0)
        by_chunk = jnp.sum(jnp.where(eye, square, 0.0).reshape(ta, ch, ch), axis=1)
        sq_ref[r, :, 0:ch] = by_chunk

        def send_sq(k, _):
            pltpu.make_async_remote_copy(
                src_ref=sq_ref.at[r],
                dst_ref=sqr_ref.at[r, k],
                send_sem=sq_sems.at[r, 0],
                recv_sem=sq_sems.at[r, 1],
                device_id=(me, (ti + k) % ta),
                device_id_type=MESH,
            ).start()
            return 0

        for i in range(nx):
            x = (my_x + i + nx // 2) % nx
            cs_ref[r, i] = gu_ref[x * NC + 1 - my_c].astype(BF16)
            pltpu.make_async_remote_copy(
                src_ref=cs_ref.at[r, i],
                dst_ref=cr_ref.at[r, i],
                send_sem=c_send.at[r],
                recv_sem=c_core.at[r, i],
                device_id=(me, my_x * NC + 1 - my_c),
                device_id_type=MESH,
            ).start()
        lax.fori_loop(1, ta, send_sq, 0)
        total = jnp.zeros((ch, feat), F32)
        for i in range(nx):
            dx = (i + nx // 2) % nx
            x = (my_x + dx) % nx
            landed = cr_ref.at[r, i]
            pltpu.make_async_copy(landed, landed, c_core.at[r, i]).wait()
            chip_sum = gu_ref[x * NC + my_c] + cr_ref[r, i].astype(F32)
            if dx == 0:
                total = chip_sum
            else:
                xs_ref[r, dx - 1] = chip_sum.astype(BF16)
                pltpu.make_async_remote_copy(
                    src_ref=xs_ref.at[r, dx - 1],
                    dst_ref=xr_ref.at[r, dx - 1],
                    send_sem=c_send.at[r],
                    recv_sem=c_x.at[r],
                    device_id=(me, x * NC + my_c),
                    device_id_type=MESH,
                ).start()
        others = sqr_ref.at[r, pl.ds(1, ta - 1)]
        pltpu.make_async_copy(others, others, sq_sems.at[r, 1]).wait()
        sq_row = sq_ref[r, pl.ds(ti, 1), 0:ch]
        for k in range(1, ta):
            sq_row += sqr_ref[r, k, pl.ds(ti, 1), 0:ch]
        sq_col = jnp.sum(jnp.where(eye[:ch], sq_row, 0.0), axis=1, keepdims=True)
        row_scale = lax.rsqrt(sq_col / (feat * ta) + 1e-5)
        pltpu.make_async_copy(xr_ref.at[r], xr_ref.at[r], c_x.at[r]).wait()
        for i in range(nx - 1):
            total += xr_ref[r, i].astype(F32)
        total = total * row_scale
        acted = jax.nn.silu(total) * pltpu.roll(total, feat - ffd, 1)
        fpad = h_ref.shape[3]
        acted = jnp.where(iota((ch, fpad), 1) < ffd, acted[:, :fpad], 0.0)
        h_ref[r, ti] = acted.astype(BF16)

        for dx in (nx // 2, *[d for d in range(1, nx) if d != nx // 2]):
            pltpu.make_async_remote_copy(
                src_ref=h_ref.at[r, ti],
                dst_ref=h_ref.at[r, ti],
                send_sem=h_send.at[r],
                recv_sem=h_x.at[r, dx],
                device_id=(me, (my_x + dx) % nx * NC + my_c),
                device_id_type=MESH,
            ).start()
        for dx in (0, *[d for d in range(1, nx) if d != nx // 2], nx // 2):
            mine = (my_x + nx - dx) % nx * NC + my_c
            block = h_ref.at[r, mine]
            if dx:
                pltpu.make_async_copy(block, block, h_x.at[r, dx]).wait()
            pltpu.make_async_remote_copy(
                src_ref=block,
                dst_ref=block,
                send_sem=h_send.at[r],
                recv_sem=h_core.at[r],
                device_id=(me, my_x * NC + 1 - my_c),
                device_id_type=MESH,
            ).start()
        landed = h_ref.at[r, pl.ds(0, nx)]
        pltpu.make_async_copy(landed, landed, h_core.at[r]).wait()

        for m in range(2):
            hid = h_ref[r, pl.ds(m * (ta // 2), ta // 2)].reshape(half, fpad)
            down = jnp.dot(hid, d_ref[r], preferred_element_type=F32)
            down = down.reshape(inst // 2, NSTEP, feat)
            part_ref[pl.ds(m * (inst // 2), inst // 2)] = down
            s_ref[r, pl.ds(m * (inst // 2), inst // 2)] = down.astype(BF16)

        def send_y(j, _):
            k = jnp.where(j % 2 == 1, nz // 2 - j // 2, nz // 2 + j // 2)
            k = jnp.where(j == nz, 0, k)
            z = (my_z + k) % nz
            for dy in range(1, ny):
                y = (my_y + dy) % ny
                pltpu.make_async_remote_copy(
                    src_ref=s_ref.at[r, y * nz + z],
                    dst_ref=yr_ref.at[r, k, dy - 1],
                    send_sem=r_send.at[r],
                    recv_sem=r_y.at[r, k],
                    device_id=gdev(y, my_z),
                    device_id_type=MESH,
                ).start()
            return 0

        lax.fori_loop(1, nz + 1, send_y, 0)

        def column_sum(k):
            landed = yr_ref.at[r, k]
            pltpu.make_async_copy(landed, landed, r_y.at[r, k]).wait()
            acc = part_ref[my_y * nz + (my_z + k) % nz]
            for dy in range(ny - 1):
                acc += yr_ref[r, k, dy].astype(F32)
            return acc

        def reduce_y(j, _):
            k = jnp.where(j % 2 == 1, nz // 2 - j // 2, nz // 2 + j // 2)
            zs_ref[r, k] = column_sum(k).astype(BF16)
            pltpu.make_async_remote_copy(
                src_ref=zs_ref.at[r, k],
                dst_ref=zr_ref.at[r, k],
                send_sem=r_send.at[r],
                recv_sem=r_z.at[r],
                device_id=gdev(my_y, (my_z + k) % nz),
                device_id_type=MESH,
            ).start()
            return 0

        lax.fori_loop(1, nz, reduce_y, 0)
        acc = column_sum(0)
        landed = zr_ref.at[r, pl.ds(1, nz - 1)]
        pltpu.make_async_copy(landed, landed, r_z.at[r]).wait()
        for k in range(1, nz):
            acc += zr_ref[r, k].astype(F32)
        node_ref[r + 1, me] = (node_ref[r, me].astype(F32) + acc).astype(BF16)
        return 0

    lax.fori_loop(0, ROUNDS, one_round, 0)
    out_ref[...] = node_ref[ROUNDS, me]

    sent = kv_send.at[pl.ds(0, gx - 1)]
    pltpu.make_async_copy(sent, sent, kv_sems.at[0]).wait()

    @pl.when(has_q)
    def _():
        gone = q_send.at[pl.ds(0, gx - 1)]
        pltpu.make_async_copy(gone, gone, q_sems.at[0]).wait()

    def drain(r, _):
        n_out = nz - 1 + nz * (ny - 1)
        blocks = node_ref.at[0, pl.ds(0, n_out)]
        pltpu.make_async_copy(blocks, blocks, n_send.at[r]).wait()
        pltpu.make_async_copy(blocks, blocks, r_send.at[r]).wait()
        pltpu.make_async_copy(cs_ref.at[r], cs_ref.at[r], c_send.at[r]).wait()
        pltpu.make_async_copy(xs_ref.at[r], xs_ref.at[r], c_send.at[r]).wait()
        others = sqr_ref.at[r, pl.ds(1, ta - 1)]
        pltpu.make_async_copy(others, others, sq_sems.at[r, 0]).wait()
        hid = h_ref.at[r, pl.ds(0, 2 * nx - 1)]
        pltpu.make_async_copy(hid, hid, h_send.at[r]).wait()
        return 0

    lax.fori_loop(0, ROUNDS, drain, 0)


def per_device(
    query_vecs,
    key_vecs,
    value_vecs,
    slot_map,
    edge_list,
    edge_types,
    type_gain,
    norm_gain,
    gate_proj,
    up_proj,
    down_proj,
):
    gx, ta = lax.axis_size("gx"), lax.axis_size("ta")
    pairs, inst, feat = query_vecs.shape
    ffd = gate_proj.shape[2]
    fpad = pl.cdiv(ffd, 128) * 128
    rows = inst * NSTEP
    nz = NZ if gx >= NZ else gx // 2
    ny = gx // nz
    nx = ta // NC
    ch = rows // ta
    edge_rows = jnp.concatenate([edge_list.T, edge_types[None]], axis=0)
    vmem = pl.BlockSpec(memory_space=pltpu.VMEM)
    hbm = pl.BlockSpec(memory_space=pl.ANY)
    dma = pltpu.SemaphoreType.DMA
    R = ROUNDS
    return pl.pallas_call(
        functools.partial(kernel, gx, ta),
        out_shape=jax.ShapeDtypeStruct((NSTEP, feat), BF16),
        in_specs=[hbm, hbm, hbm, vmem, vmem, vmem, vmem, vmem, hbm, hbm, hbm],
        out_specs=vmem,
        scratch_shapes=[
            pltpu.VMEM((3, pairs, inst, feat), BF16),
            pltpu.VMEM((inst, NSTEP, feat), BF16),
            pltpu.VMEM((inst, NSTEP, feat), BF16),
            pltpu.VMEM((inst, pairs, feat), BF16),
            pltpu.VMEM((gx // 2, pairs, feat), BF16),
            pltpu.VMEM((gx // 2 * pairs, feat), F32),
            pltpu.VMEM((2, R, feat, ffd), BF16),
            pltpu.VMEM((R, feat, feat), BF16),
            pltpu.VMEM((R, fpad, feat), BF16),
            pltpu.VMEM((ETYPES, rows, rows), BF16),
            pltpu.VMEM((rows, 128), F32),
            pltpu.VMEM((R + 1, inst, NSTEP, feat), BF16),
            pltpu.VMEM((inst, NSTEP, feat), F32),
            pltpu.VMEM((R, inst, NSTEP, feat), BF16),
            pltpu.VMEM((R, nz, ny - 1, NSTEP, feat), BF16),
            pltpu.VMEM((R, nz, NSTEP, feat), BF16),
            pltpu.VMEM((R, nz, NSTEP, feat), BF16),
            pltpu.VMEM((ta, ch, feat), F32),
            pltpu.VMEM((R, nx, ch, feat), BF16),
            pltpu.VMEM((R, nx, ch, feat), BF16),
            pltpu.VMEM((R, nx - 1, ch, feat), BF16),
            pltpu.VMEM((R, nx - 1, ch, feat), BF16),
            pltpu.VMEM((R, ta, 128), F32),
            pltpu.VMEM((R, ta, ta, 128), F32),
            pltpu.VMEM((R, ta, ch, fpad), BF16),
            dma((3,)),
            dma((3,)),
            dma((2,)),
            dma((2,)),
            dma((R,)),
            dma((R, nz)),
            dma((R,)),
            dma((R,)),
            dma((R, nz)),
            dma((R,)),
            dma((R,)),
            dma((R, nx)),
            dma((R,)),
            dma((R, 2)),
            dma((R,)),
            dma((R, nx)),
            dma((R,)),
        ],
        compiler_params=pltpu.CompilerParams(
            collective_id=0, has_side_effects=True, vmem_limit_bytes=56 << 20
        ),
    )(
        query_vecs,
        key_vecs,
        value_vecs,
        slot_map,
        edge_rows,
        edge_list,
        type_gain,
        norm_gain,
        gate_proj,
        up_proj,
        down_proj,
    )


def solution(mesh):
    placed = (
        P("gx", None, "ta"),
        P("gx", None, "ta"),
        P("gx", None, "ta"),
        P(),
        P(),
        P(),
        P(None, None, "ta"),
        P(None, "ta"),
        P(None, "ta", "gx"),
        P(None, "ta", "gx"),
        P(None, "gx", "ta"),
    )
    return jax.shard_map(
        per_device, mesh=mesh, in_specs=placed, out_specs=P("gx", "ta"), check_vma=False
    )
```

time: 1050 us -> 165 us (0.16)
  waiting for transfers between devices: 725 us -> 0 us
  blocking collectives: 236 us -> 0 us
  Pallas kernels: 0 us -> 156 us
  starting transfers between devices: 35.2 us -> 0 us
  matrix products: 14.3 us -> 0 us
  between operations: 14.1 us -> 0.01 us
    unnamed x6 -> x0, waiting for transfers between devices: 532 us -> none
    pallas_call x0 -> x1, Pallas kernels: none -> 156 us  [per_device(): pl.pallas_call(functools.partial(kernel, gx, ta), out_shape=jax.ShapeDtyp...]
    all_gather x2 -> x0, blocking collectives: 147 us -> none  [per_device(): nodes = lax.all_gather(own_rows, 'gx', axis=0, tiled=True)]
    psum x2 -> x0, waiting for transfers between devices: 133 us -> none  [per_device(): lax.psum(up_part.astype(jnp.bfloat16), 'ta').astype(jnp.float32)]
    psum x2 -> x0, blocking collectives: 89 us -> none  [per_device(): squares = lax.psum(jnp.sum(pre_norm * pre_norm, axis=-1), 'ta')]
    all_to_all x3 -> x0, waiting for transfers between devices: 59.7 us -> none  [the longest x1 20.9 us: per_device(): lax.all_to_all(sorted_queries, 'gx', split_axis=1, concat_axis=0, tiled=T...]
    all_to_all x3 -> x0, starting transfers between devices: 35 us -> none  [the longest x1 19.4 us: per_device(): lax.all_to_all(sorted_queries, 'gx', split_axis=1, concat_axis=0, tiled=T...]
    dot_general x11 -> x0, matrix products: 13.8 us -> none  [the longest x2 5.7 us: settle_rows(): jnp.dot(hidden, down_local, preferred_element_type=jnp.float32)]
  transfers between devices with their start and end apart: 7 -> 0, of which waited for: 7 -> 0; matrix products, arithmetic and copies ran while one was open for 0% -> 0% of each run, Pallas kernels for 0% -> 0%
where the time goes in v1:
time: 165 us; the launch traced here: 164 us
  Pallas kernels  156 us (95%)
  local copies, waits for them, and re-layouts  7.73 us (5%)
    pallas_call x1, Pallas kernels, per_device(): pl.pallas_call(functools.partial(kernel, gx, ta), out_shape=jax.ShapeDtyp...  156 us
    unnamed x11, local copies, waits for them, and re-layouts  7.73 us

profile of v1, /device:TPU:1, one launch (start us, length us, event | category | flops | bytes accessed | tf_op | source)
XLA Modules:
  0.0 164.3 jit_solution(15318985233195185488)
XLA Ops:
  0.0 0.0 copy-start.1
  0.0 0.0 copy-start.2
  0.0 0.7 copy-done.1
  0.7 0.0 copy-done.2
  0.7 0.6 pad_add_fusion.edge_rows_ref
  1.3 1.3 copy.13.tgain_ref
  2.6 0.8 copy.12.edge_cols_ref
  3.4 0.0 copy-start
  3.4 2.3 %copy.14.g_hbm = bf16[2,640,320]{2,1,0:T(8,128)(2,1)} copy(bf16[2,640,320]{1,2,0:T(8,128)(2,1)} %param.19) | data formatting | bytes 1638400 | tf_op args[8]
  5.7 0.0 copy-done
  5.7 1.3 copy.15.u_hbm
  7.0 156.0 %shard_map.109 = bf16[8,640]{1,0:T(8,128)(2,1)} custom-call(bf16[4,64,640]{2,1,0:T(8,128)(2,1)} %q_hbm.1, bf16[4,64,640]{2,1,0:T(8,128)(2,1)} %k_hbm.1, bf16[4,64,640]{2,1,0:T(8,128)(2,1)} %v_hbm.1, s32[16,64]{1,0:T(8,128)} %slot_ref.1, s32[3,256]{1,0:T(4,128)} %pad_add_fusion.edge_rows_ref, s32[256,2]{1,0:T(8,128)} %copy.12.edge_cols_ref, ...), custom_call_target="tpu_custom_call" | custom-call | tf_op jit(solution)/shard_map/pallas_call | solution.py:515
  163.0 1.3 copy.17
Async XLA Ops:
  0.0 0.7 copy-start.1
  0.0 0.7 copy-start.2
  3.4 2.3 %copy-start = (bf16[2,640,320]{1,2,0:T(8,128)(2,1)S(1)}, bf16[2,640,320]{1,2,0:T(8,128)(2,1)}, u32[]{:S(2)}) copy-start(bf16[2,640,320]{1,2,0:T(8,128)(2,1)} %param.20) | copy-start | bytes 2457604

commit v2 on v1

--- a/solution.py
+++ b/solution.py
@@ -18,6 +18,7 @@
 NC = 2
 F32 = jnp.float32
 BF16 = jnp.bfloat16
+NT = (((1,), (1,)), ((), ()))
 
 
 def iota(shape, dim):
@@ -31,8 +32,8 @@
     k_hbm,
     v_hbm,
     slot_ref,
-    edge_rows_ref,
-    edge_cols_ref,
+    edge_ref,
+    type_ref,
     tgain_ref,
     ngain_ref,
     g_hbm,
@@ -45,7 +46,6 @@
     q_send,
     q_recv,
     q_f32,
-    gu_in,
     w_ref,
     d_ref,
     adj_ref,
@@ -64,10 +64,13 @@
     sq_ref,
     sqr_ref,
     h_ref,
+    square_ref,
     in_sem,
     w_sem,
     kv_sems,
     q_sems,
+    kv_send_sem,
+    q_send_sem,
     n_send,
     n_z,
     n_y,
@@ -92,6 +95,8 @@
     rows = inst * NSTEP
     ch = rows // ta
     half = rows // 2
+    c0 = (heads + 1) // 2 * HEAD
+    cuts = (pl.ds(0, c0), pl.ds(c0, feat - c0))
     me = lax.axis_index("gx")
     ti = lax.axis_index("ta")
     my_y, my_z = me // nz, me % nz
@@ -126,12 +131,10 @@
     loads[2].start()
     loads[0].start()
     weights = [
-        pltpu.make_async_copy(g_hbm, gu_in.at[0], w_sem.at[0]),
-        pltpu.make_async_copy(u_hbm, gu_in.at[1], w_sem.at[1]),
+        pltpu.make_async_copy(g_hbm, w_ref.at[:, pl.ds(0, ffd)], w_sem.at[0]),
+        pltpu.make_async_copy(u_hbm, w_ref.at[:, pl.ds(ffd, ffd)], w_sem.at[1]),
         pltpu.make_async_copy(d_hbm, d_ref.at[:, pl.ds(0, ffd)], w_sem.at[2]),
     ]
-    for w in weights:
-        w.start()
 
     order = slot_ref[pl.ds(me * PD // STEPS, 1), :].astype(F32)
     r8 = iota((rows, inst), 0)
@@ -163,160 +166,175 @@
 
     has_q = me % 4 >= 2
 
-    @pl.when(has_q)
-    def _():
-        def send_q(k, _):
+    for c, cut in enumerate(cuts):
+
+        @pl.when(has_q)
+        def _(c=c, cut=cut):
+            def send_q(k, _):
+                dest = (me + k) % gx
+                pltpu.make_async_remote_copy(
+                    src_ref=q_send.at[dest, :, cut],
+                    dst_ref=q_recv.at[q_slot(me), :, cut],
+                    send_sem=q_send_sem.at[0],
+                    recv_sem=q_sems.at[c],
+                    device_id=(dest, ti),
+                    device_id_type=MESH,
+                ).start()
+                return 0
+
+            lax.fori_loop(1, gx, send_q, 0)
+            pltpu.make_async_copy(
+                q_send.at[me, :, cut], q_recv.at[q_slot(me), :, cut], q_sems.at[c]
+            ).start()
+
+        def send_kv(k, _, c=c, cut=cut):
             dest = (me + k) % gx
             pltpu.make_async_remote_copy(
-                src_ref=q_send.at[dest],
-                dst_ref=q_recv.at[q_slot(me)],
-                send_sem=q_sems.at[0],
-                recv_sem=q_sems.at[1],
+                src_ref=kv_send.at[dest, :, cut],
+                dst_ref=kv_recv.at[me, :, cut],
+                send_sem=kv_send_sem.at[0],
+                recv_sem=kv_sems.at[c],
                 device_id=(dest, ti),
                 device_id_type=MESH,
             ).start()
             return 0
 
-        lax.fori_loop(1, gx, send_q, 0)
+        lax.fori_loop(1, gx, send_kv, 0)
         pltpu.make_async_copy(
-            q_send.at[me], q_recv.at[q_slot(me)], q_sems.at[1]
+            kv_send.at[me, :, cut], kv_recv.at[me, :, cut], kv_sems.at[c]
         ).start()
 
-    def send_kv(k, _):
-        dest = (me + k) % gx
-        pltpu.make_async_remote_copy(
-            src_ref=kv_send.at[dest],
-            dst_ref=kv_recv.at[me],
-            send_sem=kv_sems.at[0],
-            recv_sem=kv_sems.at[1],
-            device_id=(dest, ti),
-            device_id_type=MESH,
-        ).start()
-        return 0
-
-    lax.fori_loop(1, gx, send_kv, 0)
-    pltpu.make_async_copy(kv_send.at[me], kv_recv.at[me], kv_sems.at[1]).start()
-
-    tgt = edge_rows_ref[1:2, :]
-    typ = edge_rows_ref[2:3, :]
-    src = edge_cols_ref[:, 0:1]
+    for w in weights:
+        w.start()
+    src = edge_ref[0:1, :]
+    tgt = edge_ref[1:2, :]
+    typ = type_ref[...]
     edges = tgt.shape[1]
-    at_target = iota((rows, edges), 0) // NSTEP == tgt
-    at_source = jnp.where(src == iota((edges, rows), 1) // NSTEP, 1.0, 0.0).astype(BF16)
+    inst_of = iota((rows, edges), 0) // NSTEP
+    at_target = inst_of == tgt
+    at_source = jnp.where(inst_of == src, 1.0, 0.0).astype(BF16)
     same_step = iota((rows, rows), 0) % NSTEP == iota((rows, rows), 1) % NSTEP
     for t in range(ETYPES):
         hit = jnp.where(at_target & (typ == t), 1.0, 0.0).astype(BF16)
-        count = jnp.dot(hit, at_source, preferred_element_type=F32)
+        count = lax.dot_general(hit, at_source, NT, preferred_element_type=F32)
         adj_ref[t] = jnp.where(same_step, count, 0.0).astype(BF16)
     degree = jnp.sum(jnp.where(at_target, 1.0, 0.0), axis=1, keepdims=True)
     deg_ref[...] = jnp.broadcast_to(jnp.maximum(degree, 1.0), deg_ref.shape)
-
+    if d_ref.shape[1] > ffd:
+        d_ref[:, ffd:, :] = jnp.zeros((ROUNDS, d_ref.shape[1] - ffd, feat), BF16)
     for w in weights:
         w.wait()
-    left = jnp.where(iota((ffd, feat), 0) == iota((ffd, feat), 1), 1.0, 0.0).astype(BF16)
-    right = jnp.where(iota((ffd, feat), 0) + ffd == iota((ffd, feat), 1), 1.0, 0.0)
-    right = right.astype(BF16)
-
-    def place(r, _):
-        w_ref[r] = (
-            jnp.dot(gu_in[0, r], left, preferred_element_type=F32)
-            + jnp.dot(gu_in[1, r], right, preferred_element_type=F32)
-        ).astype(BF16)
-        if d_ref.shape[1] > ffd:
-            d_ref[r, ffd:, :] = jnp.zeros((d_ref.shape[1] - ffd, feat), BF16)
-        return 0
-
-    lax.fori_loop(0, ROUNDS, place, 0)
-
-    pltpu.make_async_copy(q_recv, q_recv, q_sems.at[1]).wait()
-    for j in range(q_recv.shape[0]):
-        q_f32[j * PD : (j + 1) * PD, :] = q_recv[j].astype(F32)
-    q_all = q_f32[...].astype(BF16)
-    pltpu.make_async_copy(kv_recv, kv_recv, kv_sems.at[1]).wait()
-    kv_all = kv_recv[...].astype(F32).reshape(rows, feat).astype(BF16)
-    nq = q_all.shape[0]
+
+    nq = q_f32.shape[0]
     lane = iota((nq, rows), 1)
     key_step = (lane // NSTEP) % 4 * PD + lane % NSTEP
     q_step = iota((nq, rows), 0) % NSTEP + (STEPS - NSTEP)
     allowed = (lane % NSTEP < PD) & (key_step <= q_step)
-    pooled = []
-    for h in range(heads):
-        cut = slice(h * HEAD, (h + 1) * HEAD)
-        scores = lax.dot_general(
-            q_all[:, cut],
-            kv_all[:, cut],
-            (((1,), (1,)), ((), ())),
-            preferred_element_type=F32,
-        ) * (1.0 / HEAD**0.5)
-        scores = jnp.where(allowed, scores, -1e30)
-        expd = jnp.exp(scores - jnp.max(scores, axis=1, keepdims=True))
-        probs = expd / jnp.sum(expd, axis=1, keepdims=True)
-        probs = pltpu.roll(probs, PD, 1).astype(BF16)
-        att = jnp.dot(probs, kv_all[:, cut], preferred_element_type=F32)
-        pooled.append(jnp.mean(att.reshape(nq // NSTEP, NSTEP, HEAD), axis=0))
-    node_ref[0, me] = jnp.concatenate(pooled, axis=1).astype(BF16)
+
+    def attend(c, cut):
+        whole = q_recv.at[:, :, cut]
+        pltpu.make_async_copy(whole, whole, q_sems.at[c]).wait()
+        for j in range(q_recv.shape[0]):
+            q_f32[j * PD : (j + 1) * PD, cut] = q_recv[j, :, cut].astype(F32)
+        q_all = q_f32[:, cut].astype(BF16)
+        whole = kv_recv.at[:, :, cut]
+        pltpu.make_async_copy(whole, whole, kv_sems.at[c]).wait()
+        width = cut.size
+        kv_all = kv_recv[:, :, cut].astype(F32).reshape(rows, width).astype(BF16)
+        pooled = []
+        for h in range(width // HEAD):
+            own = slice(h * HEAD, (h + 1) * HEAD)
+            scores = lax.dot_general(
+                q_all[:, own], kv_all[:, own], NT, preferred_element_type=F32
+            ) * (1.0 / HEAD**0.5)
+            scores = jnp.where(allowed, scores, -1e30)
+            expd = jnp.exp(scores - jnp.max(scores, axis=1, keepdims=True))
+            probs = expd / jnp.sum(expd, axis=1, keepdims=True)
+            probs = pltpu.roll(probs, PD, 1).astype(BF16)
+            att = jnp.dot(probs, kv_all[:, own], preferred_element_type=F32)
+            pooled.append(jnp.mean(att.reshape(nq // NSTEP, NSTEP, HEAD), axis=0))
+        node_ref[0, me, :, cut] = jnp.concatenate(pooled, axis=1).astype(BF16)
 
     eye = iota((rows, ch), 0) % ch == iota((rows, ch), 1)
 
-    def one_round(r, _):
-        nodes = node_ref.at[r]
-
-        def send_z(j, _):
-            k = jnp.where(j % 2 == 1, nz // 2 - j // 2, nz // 2 + j // 2)
-            pltpu.make_async_remote_copy(
-                src_ref=nodes.at[me],
-                dst_ref=nodes.at[me],
-                send_sem=n_send.at[r],
-                recv_sem=n_z.at[r, k],
-                device_id=gdev(my_y, (my_z + k) % nz),
-                device_id_type=MESH,
-            ).start()
-            return 0
-
-        lax.fori_loop(1, nz, send_z, 0)
-
-        def pass_on(blk):
-            for dy in range(1, ny):
+    if nz == 16:
+        first = (8, 5, 11, 2, 14, 1, 15)
+        second = {5: (2, 14, 1, 15), 11: (2, 14, 1, 15)}
+        arrivals = (1, 15, 2, 14, 5, 11, 4, 6, 10, 12, 3, 7, 9, 13, 8)
+    else:
+        first = arrivals = tuple(range(1, nz))
+        second = {}
+
+    def pass_on(r, s, cut, blk):
+        for dy in (2, 1, 3):
+            if dy < ny:
                 pltpu.make_async_remote_copy(
-                    src_ref=nodes.at[blk],
-                    dst_ref=nodes.at[blk],
-                    send_sem=n_send.at[r],
-                    recv_sem=n_y.at[r],
+                    src_ref=node_ref.at[r, blk, :, cut],
+                    dst_ref=node_ref.at[r, blk, :, cut],
+                    send_sem=n_send.at[s],
+                    recv_sem=n_y.at[s],
                     device_id=gdev((my_y + dy) % ny, my_z),
                     device_id_type=MESH,
                 ).start()
 
-        pass_on(me)
-
-        def forward(j, _):
-            k = jnp.where(j % 2 == 1, (j + 1) // 2, nz - j // 2)
+    def send_z(r, s, cut, blk, step, total):
+        pltpu.make_async_remote_copy(
+            src_ref=node_ref.at[r, blk, :, cut],
+            dst_ref=node_ref.at[r, blk, :, cut],
+            send_sem=n_send.at[s],
+            recv_sem=n_z.at[s, total],
+            device_id=gdev(my_y, (my_z + step) % nz),
+            device_id_type=MESH,
+        ).start()
+
+    def gather_start(r, s, cut):
+        for k in first:
+            send_z(r, s, cut, me, k, k)
+        pass_on(r, s, cut, me)
+
+    def gather_forward(r, s, cut):
+        for k in arrivals:
             blk = my_y * nz + (my_z + nz - k) % nz
-            pltpu.make_async_copy(nodes.at[blk], nodes.at[blk], n_z.at[r, k]).wait()
-            pass_on(blk)
-            return 0
-
-        lax.fori_loop(1, nz, forward, 0)
-        arrived = nodes.at[pl.ds(0, (ny - 1) * nz)]
-        pltpu.make_async_copy(arrived, arrived, n_y.at[r]).wait()
-
-        node_f32 = nodes[...].astype(F32).reshape(rows, feat)
+            landed = node_ref.at[r, blk, :, cut]
+            pltpu.make_async_copy(landed, landed, n_z.at[s, k]).wait()
+            for more in second.get(k, ()):
+                send_z(r, s, cut, blk, more, (k + more) % nz)
+            pass_on(r, s, cut, blk)
+
+    def gather_end(r, s, cut):
+        arrived = node_ref.at[r, pl.ds(0, (ny - 1) * nz), :, cut]
+        pltpu.make_async_copy(arrived, arrived, n_y.at[s]).wait()
+
+    def mix(r, c, cut):
+        width = cut.size
+        node_f32 = node_ref[r, :, :, cut].astype(F32).reshape(rows, width)
         node_all = node_f32.astype(BF16)
-        tgain = tgain_ref[r]
-        squares = []
+        ngain = ngain_ref[pl.ds(r, 1), cut]
+        weight = w_ref[r, :, cut]
         for m in range(2):
             mine = slice(m * half, (m + 1) * half)
-            total = jnp.zeros((half, feat), F32)
+            total = jnp.zeros((half, width), F32)
             for t in range(ETYPES):
-                total += tgain[t : t + 1] * jnp.dot(
+                total += tgain_ref[t, pl.ds(r, 1), cut] * jnp.dot(
                     adj_ref[t, mine, :], node_all, preferred_element_type=F32
                 )
             pre = node_f32[mine] + total / deg_ref[mine, 0:1]
-            squares.append(jnp.sum(pre * pre, axis=1, keepdims=True))
-            scaled = (pre * ngain_ref[pl.ds(r, 1), :]).astype(BF16)
-            gu_ref[pl.ds(m * (ta // 2), ta // 2)] = jnp.dot(
-                scaled, w_ref[r], preferred_element_type=F32
-            ).reshape(ta // 2, ch, feat)
-        square = jnp.concatenate(squares, axis=0)
+            square = jnp.sum(pre * pre, axis=1, keepdims=True)
+            square = jnp.broadcast_to(square, (half, 128))
+            scaled = (pre * ngain).astype(BF16)
+            sums = lax.dot_general(scaled, weight, NT, preferred_element_type=F32)
+            sums = sums.reshape(ta // 2, ch, feat)
+            spot = slice(m * (ta // 2), (m + 1) * (ta // 2))
+            if c == 0:
+                gu_ref[spot] = sums
+                square_ref[mine] = square
+            else:
+                gu_ref[spot] += sums
+                square_ref[mine] += square
+
+    def one_round(r, _):
+        mix(r, 1, cuts[1])
+        square = square_ref[:, 0:1]
         by_chunk = jnp.sum(jnp.where(eye, square, 0.0).reshape(ta, ch, ch), axis=1)
         sq_ref[r, :, 0:ch] = by_chunk
 
@@ -456,23 +474,46 @@
         for k in range(1, nz):
             acc += zr_ref[r, k].astype(F32)
         node_ref[r + 1, me] = (node_ref[r, me].astype(F32) + acc).astype(BF16)
+
+        @pl.when(r + 1 < ROUNDS)
+        def _():
+            for c, cut in enumerate(cuts):
+                gather_start(r + 1, 2 + c, cut)
+            for c, cut in enumerate(cuts):
+                gather_forward(r + 1, 2 + c, cut)
+            gather_end(r + 1, 2, cuts[0])
+            mix(r + 1, 0, cuts[0])
+            gather_end(r + 1, 3, cuts[1])
+
         return 0
 
+    attend(0, cuts[0])
+    gather_start(0, 0, cuts[0])
+    gather_forward(0, 0, cuts[0])
+    attend(1, cuts[1])
+    gather_start(0, 1, cuts[1])
+    gather_forward(0, 1, cuts[1])
+    gather_end(0, 0, cuts[0])
+    mix(0, 0, cuts[0])
+    gather_end(0, 1, cuts[1])
     lax.fori_loop(0, ROUNDS, one_round, 0)
     out_ref[...] = node_ref[ROUNDS, me]
 
     sent = kv_send.at[pl.ds(0, gx - 1)]
-    pltpu.make_async_copy(sent, sent, kv_sems.at[0]).wait()
+    pltpu.make_async_copy(sent, sent, kv_send_sem.at[0]).wait()
 
     @pl.when(has_q)
     def _():
         gone = q_send.at[pl.ds(0, gx - 1)]
-        pltpu.make_async_copy(gone, gone, q_sems.at[0]).wait()
+        pltpu.make_async_copy(gone, gone, q_send_sem.at[0]).wait()
+
+    n_out = nz - 1 + nz * (ny - 1)
+    for s in range(2 * ROUNDS):
+        blocks = node_ref.at[0, pl.ds(0, n_out), :, cuts[s % 2]]
+        pltpu.make_async_copy(blocks, blocks, n_send.at[s]).wait()
 
     def drain(r, _):
-        n_out = nz - 1 + nz * (ny - 1)
         blocks = node_ref.at[0, pl.ds(0, n_out)]
-        pltpu.make_async_copy(blocks, blocks, n_send.at[r]).wait()
         pltpu.make_async_copy(blocks, blocks, r_send.at[r]).wait()
         pltpu.make_async_copy(cs_ref.at[r], cs_ref.at[r], c_send.at[r]).wait()
         pltpu.make_async_copy(xs_ref.at[r], xs_ref.at[r], c_send.at[r]).wait()
@@ -507,7 +548,6 @@
     ny = gx // nz
     nx = ta // NC
     ch = rows // ta
-    edge_rows = jnp.concatenate([edge_list.T, edge_types[None]], axis=0)
     vmem = pl.BlockSpec(memory_space=pltpu.VMEM)
     hbm = pl.BlockSpec(memory_space=pl.ANY)
     dma = pltpu.SemaphoreType.DMA
@@ -524,7 +564,6 @@
             pltpu.VMEM((inst, pairs, feat), BF16),
             pltpu.VMEM((gx // 2, pairs, feat), BF16),
             pltpu.VMEM((gx // 2 * pairs, feat), F32),
-            pltpu.VMEM((2, R, feat, ffd), BF16),
             pltpu.VMEM((R, feat, feat), BF16),
             pltpu.VMEM((R, fpad, feat), BF16),
             pltpu.VMEM((ETYPES, rows, rows), BF16),
@@ -543,13 +582,16 @@
             pltpu.VMEM((R, ta, 128), F32),
             pltpu.VMEM((R, ta, ta, 128), F32),
             pltpu.VMEM((R, ta, ch, fpad), BF16),
+            pltpu.VMEM((rows, 128), F32),
             dma((3,)),
             dma((3,)),
             dma((2,)),
             dma((2,)),
-            dma((R,)),
-            dma((R, nz)),
-            dma((R,)),
+            dma((1,)),
+            dma((1,)),
+            dma((2 * R,)),
+            dma((2 * R, nz)),
+            dma((2 * R,)),
             dma((R,)),
             dma((R, nz)),
             dma((R,)),
@@ -569,12 +611,12 @@
         key_vecs,
         value_vecs,
         slot_map,
-        edge_rows,
-        edge_list,
-        type_gain,
+        edge_list.T,
+        edge_types[None],
+        jnp.swapaxes(type_gain, 0, 1),
         norm_gain,
-        gate_proj,
-        up_proj,
+        jnp.swapaxes(gate_proj, 1, 2),
+        jnp.swapaxes(up_proj, 1, 2),
         down_proj,
     )
 

time: 165 us -> 155 us (0.939)
  local copies, waits for them, and re-layouts: 7.73 us -> 1.3 us
  Pallas kernels: 156 us -> 154 us
    unnamed x11 -> x1, local copies, waits for them, and re-layouts: 7.73 us -> 1.3 us
    pallas_call x1, Pallas kernels: 156 us -> 154 us  [per_device(): pl.pallas_call(functools.partial(kernel, gx, ta), out_shape=jax.ShapeDtyp...]
where the time goes in v2:
time: 155 us
  Pallas kernels  154 us (99%)
    pallas_call x1, Pallas kernels, per_device(): pl.pallas_call(functools.partial(kernel, gx, ta), out_shape=jax.ShapeDtyp...  154 us

profile of v2, /device:TPU:1, one launch (start us, length us, event | category | flops | bytes accessed | tf_op | source)
XLA Modules:
  0.0 154.9 jit_solution(1149611639846186841)
XLA Ops:
  0.0 153.6 %shard_map.109 = bf16[8,640]{1,0:T(8,128)(2,1)} custom-call(bf16[4,64,640]{2,1,0:T(8,128)(2,1)} %q_hbm.1, bf16[4,64,640]{2,1,0:T(8,128)(2,1)} %k_hbm.1, bf16[4,64,640]{2,1,0:T(8,128)(2,1)} %v_hbm.1, s32[16,64]{1,0:T(8,128)} %slot_ref.1, s32[2,256]{1,0:T(2,128)} %bitcast.8, s32[1,256]{1,0:T(1,128)} %bitcast.9, f32[3,2,640]{2,1,0:T(2,128)} %bitcast.7, ...), custom_call_target="tpu_custom_call" | custom-call | tf_op jit(solution)/shard_map/pallas_call | solution.py:555
  153.6 1.3 copy.13

commit v3 on v2

--- a/solution.py
+++ b/solution.py
@@ -161,6 +161,12 @@
     )
     pl.semaphore_wait(barrier, gx - 1 + ta - 1)
 
+    def partner(k):
+        n = k - 1
+        turn, dy = n // ny, (n + 1) % ny
+        step = jnp.where(turn % 2 == 1, nz // 2 - (turn + 1) // 2, nz // 2 + turn // 2)
+        return (my_y + dy) % ny * nz + (my_z + step) % nz
+
     def q_slot(g):
         return (g // 4) * 2 + g % 4 - 2
 
@@ -171,7 +177,7 @@
         @pl.when(has_q)
         def _(c=c, cut=cut):
             def send_q(k, _):
-                dest = (me + k) % gx
+                dest = partner(k)
                 pltpu.make_async_remote_copy(
                     src_ref=q_send.at[dest, :, cut],
                     dst_ref=q_recv.at[q_slot(me), :, cut],
@@ -188,7 +194,7 @@
             ).start()
 
         def send_kv(k, _, c=c, cut=cut):
-            dest = (me + k) % gx
+            dest = partner(k)
             pltpu.make_async_remote_copy(
                 src_ref=kv_send.at[dest, :, cut],
                 dst_ref=kv_recv.at[me, :, cut],
@@ -258,9 +264,9 @@
     eye = iota((rows, ch), 0) % ch == iota((rows, ch), 1)
 
     if nz == 16:
-        first = (8, 5, 11, 2, 14, 1, 15)
-        second = {5: (2, 14, 1, 15), 11: (2, 14, 1, 15)}
-        arrivals = (1, 15, 2, 14, 5, 11, 4, 6, 10, 12, 3, 7, 9, 13, 8)
+        first = (8, 7, 9, 6, 10, 5, 11, 4, 12, 3, 13, 2, 14, 1, 15)
+        second = {}
+        arrivals = first[::-1]
     else:
         first = arrivals = tuple(range(1, nz))
         second = {}
@@ -334,9 +340,6 @@
 
     def one_round(r, _):
         mix(r, 1, cuts[1])
-        square = square_ref[:, 0:1]
-        by_chunk = jnp.sum(jnp.where(eye, square, 0.0).reshape(ta, ch, ch), axis=1)
-        sq_ref[r, :, 0:ch] = by_chunk
 
         def send_sq(k, _):
             pltpu.make_async_remote_copy(
@@ -360,6 +363,9 @@
                 device_id=(me, my_x * NC + 1 - my_c),
                 device_id_type=MESH,
             ).start()
+        square = square_ref[:, 0:1]
+        by_chunk = jnp.sum(jnp.where(eye, square, 0.0).reshape(ta, ch, ch), axis=1)
+        sq_ref[r, :, 0:ch] = by_chunk
         lax.fori_loop(1, ta, send_sq, 0)
         total = jnp.zeros((ch, feat), F32)
         for i in range(nx):
@@ -489,9 +495,9 @@
 
     attend(0, cuts[0])
     gather_start(0, 0, cuts[0])
-    gather_forward(0, 0, cuts[0])
     attend(1, cuts[1])
     gather_start(0, 1, cuts[1])
+    gather_forward(0, 0, cuts[0])
     gather_forward(0, 1, cuts[1])
     gather_end(0, 0, cuts[0])
     mix(0, 0, cuts[0])

time: 155 us -> 150 us (0.968)
  Pallas kernels: 154 us -> 148 us
    pallas_call x1, Pallas kernels: 154 us -> 148 us  [per_device(): pl.pallas_call(functools.partial(kernel, gx, ta), out_shape=jax.ShapeDtyp...]
where the time goes in v3:
time: 150 us
  Pallas kernels  148 us (99%)
    pallas_call x1, Pallas kernels, per_device(): pl.pallas_call(functools.partial(kernel, gx, ta), out_shape=jax.ShapeDtyp...  148 us

profile of v3, /device:TPU:1, one launch (start us, length us, event | category | flops | bytes accessed | tf_op | source)
XLA Modules:
  0.0 149.5 jit_solution(13740262458305387612)
XLA Ops:
  0.0 148.2 %shard_map.109 = bf16[8,640]{1,0:T(8,128)(2,1)} custom-call(bf16[4,64,640]{2,1,0:T(8,128)(2,1)} %q_hbm.1, bf16[4,64,640]{2,1,0:T(8,128)(2,1)} %k_hbm.1, bf16[4,64,640]{2,1,0:T(8,128)(2,1)} %v_hbm.1, s32[16,64]{1,0:T(8,128)} %slot_ref.1, s32[2,256]{1,0:T(2,128)} %bitcast.8, s32[1,256]{1,0:T(1,128)} %bitcast.9, f32[3,2,640]{2,1,0:T(2,128)} %bitcast.7, ...), custom_call_target="tpu_custom_call" | custom-call | tf_op jit(solution)/shard_map/pallas_call | solution.py:561
  148.2 1.3 copy.13

commit v4 on v3

--- a/solution.py
+++ b/solution.py
@@ -434,57 +434,65 @@
             part_ref[pl.ds(m * (inst // 2), inst // 2)] = down
             s_ref[r, pl.ds(m * (inst // 2), inst // 2)] = down.astype(BF16)
 
-        def send_y(j, _):
-            k = jnp.where(j % 2 == 1, nz // 2 - j // 2, nz // 2 + j // 2)
-            k = jnp.where(j == nz, 0, k)
-            z = (my_z + k) % nz
-            for dy in range(1, ny):
-                y = (my_y + dy) % ny
+        for c, cut in enumerate(cuts):
+
+            def send_y(j, _, c=c, cut=cut):
+                k = jnp.where(j % 2 == 1, nz // 2 - j // 2, nz // 2 + j // 2)
+                k = jnp.where(j == nz, 0, k)
+                z = (my_z + k) % nz
+                for dy in range(1, ny):
+                    y = (my_y + dy) % ny
+                    pltpu.make_async_remote_copy(
+                        src_ref=s_ref.at[r, y * nz + z, :, cut],
+                        dst_ref=yr_ref.at[r, k, dy - 1, :, cut],
+                        send_sem=r_send.at[r],
+                        recv_sem=r_y.at[2 * r + c, k],
+                        device_id=gdev(y, my_z),
+                        device_id_type=MESH,
+                    ).start()
+                return 0
+
+            lax.fori_loop(1, nz + 1, send_y, 0)
+
+        def column_sum(k, c, cut):
+            landed = yr_ref.at[r, k, :, :, cut]
+            pltpu.make_async_copy(landed, landed, r_y.at[2 * r + c, k]).wait()
+            acc = part_ref[my_y * nz + (my_z + k) % nz, :, cut]
+            for dy in range(ny - 1):
+                acc += yr_ref[r, k, dy, :, cut].astype(F32)
+            return acc
+
+        for c, cut in enumerate(cuts):
+
+            def reduce_y(j, _, c=c, cut=cut):
+                k = jnp.where(j % 2 == 1, nz // 2 - j // 2, nz // 2 + j // 2)
+                zs_ref[r, k, :, cut] = column_sum(k, c, cut).astype(BF16)
                 pltpu.make_async_remote_copy(
-                    src_ref=s_ref.at[r, y * nz + z],
-                    dst_ref=yr_ref.at[r, k, dy - 1],
+                    src_ref=zs_ref.at[r, k, :, cut],
+                    dst_ref=zr_ref.at[r, k, :, cut],
                     send_sem=r_send.at[r],
-                    recv_sem=r_y.at[r, k],
-                    device_id=gdev(y, my_z),
+                    recv_sem=r_z.at[2 * r + c],
+                    device_id=gdev(my_y, (my_z + k) % nz),
                     device_id_type=MESH,
                 ).start()
-            return 0
-
-        lax.fori_loop(1, nz + 1, send_y, 0)
-
-        def column_sum(k):
-            landed = yr_ref.at[r, k]
-            pltpu.make_async_copy(landed, landed, r_y.at[r, k]).wait()
-            acc = part_ref[my_y * nz + (my_z + k) % nz]
-            for dy in range(ny - 1):
-                acc += yr_ref[r, k, dy].astype(F32)
-            return acc
-
-        def reduce_y(j, _):
-            k = jnp.where(j % 2 == 1, nz // 2 - j // 2, nz // 2 + j // 2)
-            zs_ref[r, k] = column_sum(k).astype(BF16)
-            pltpu.make_async_remote_copy(
-                src_ref=zs_ref.at[r, k],
-                dst_ref=zr_ref.at[r, k],
-                send_sem=r_send.at[r],
-                recv_sem=r_z.at[r],
-                device_id=gdev(my_y, (my_z + k) % nz),
-                device_id_type=MESH,
-            ).start()
-            return 0
-
-        lax.fori_loop(1, nz, reduce_y, 0)
-        acc = column_sum(0)
-        landed = zr_ref.at[r, pl.ds(1, nz - 1)]
-        pltpu.make_async_copy(landed, landed, r_z.at[r]).wait()
-        for k in range(1, nz):
-            acc += zr_ref[r, k].astype(F32)
-        node_ref[r + 1, me] = (node_ref[r, me].astype(F32) + acc).astype(BF16)
+                return 0
+
+            lax.fori_loop(1, nz, reduce_y, 0)
+        for c, cut in enumerate(cuts):
+            acc = column_sum(0, c, cut)
+            landed = zr_ref.at[r, pl.ds(1, nz - 1), :, cut]
+            pltpu.make_async_copy(landed, landed, r_z.at[2 * r + c]).wait()
+            for k in range(1, nz):
+                acc += zr_ref[r, k, :, cut].astype(F32)
+            acc += node_ref[r, me, :, cut].astype(F32)
+            node_ref[r + 1, me, :, cut] = acc.astype(BF16)
+
+            @pl.when(r + 1 < ROUNDS)
+            def _(c=c, cut=cut):
+                gather_start(r + 1, 2 + c, cut)
 
         @pl.when(r + 1 < ROUNDS)
         def _():
-            for c, cut in enumerate(cuts):
-                gather_start(r + 1, 2 + c, cut)
             for c, cut in enumerate(cuts):
                 gather_forward(r + 1, 2 + c, cut)
             gather_end(r + 1, 2, cuts[0])
@@ -599,8 +607,8 @@
             dma((2 * R, nz)),
             dma((2 * R,)),
             dma((R,)),
-            dma((R, nz)),
-            dma((R,)),
+            dma((2 * R, nz)),
+            dma((2 * R,)),
             dma((R,)),
             dma((R, nx)),
             dma((R,)),

time: 150 us -> 147 us (0.980)
  Pallas kernels: 148 us -> 146 us
    pallas_call x1, Pallas kernels: 148 us -> 146 us  [per_device(): pl.pallas_call(functools.partial(kernel, gx, ta), out_shape=jax.ShapeDtyp...]
where the time goes in v4:
time: 147 us
  Pallas kernels  146 us (99%)
    pallas_call x1, Pallas kernels, per_device(): pl.pallas_call(functools.partial(kernel, gx, ta), out_shape=jax.ShapeDtyp...  146 us

profile of v4, /device:TPU:1, one launch (start us, length us, event | category | flops | bytes accessed | tf_op | source)
XLA Modules:
  0.0 147.1 jit_solution(15087164685999228663)
XLA Ops:
  0.0 145.8 %shard_map.109 = bf16[8,640]{1,0:T(8,128)(2,1)} custom-call(bf16[4,64,640]{2,1,0:T(8,128)(2,1)} %q_hbm.1, bf16[4,64,640]{2,1,0:T(8,128)(2,1)} %k_hbm.1, bf16[4,64,640]{2,1,0:T(8,128)(2,1)} %v_hbm.1, s32[16,64]{1,0:T(8,128)} %slot_ref.1, s32[2,256]{1,0:T(2,128)} %bitcast.8, s32[1,256]{1,0:T(1,128)} %bitcast.9, f32[3,2,640]{2,1,0:T(2,128)} %bitcast.7, ...), custom_call_target="tpu_custom_call" | custom-call | tf_op jit(solution)/shard_map/pallas_call | solution.py:569
  145.8 1.3 copy.13
